TPU v7x, 32 devices: a whole 2x2x4 slice. The times are simulated.
32 devices in a mesh: fsdp: 2 (over core), ctx: 4 (over y, x), tp: 4 (over z).
Axes of the slice: x: 2, y: 2, z: 4, core: 2. Of those that a mesh axis runs over, the one named last changes fastest.
Arguments:
- tokens: bfloat16 [4096, 2048], P(('fsdp', 'ctx')), may hold values from -6 to 6
- attn_gain: bfloat16 [2048], P(('fsdp', 'ctx')), may hold values from 0.099609375 to 1.8984375
- w_query: bfloat16 [2048, 2048], P(('fsdp', 'ctx'), 'tp'), may hold values from -0.125 to 0.125
- w_key: bfloat16 [2048, 256], P(('fsdp', 'ctx'), 'tp'), may hold values from -0.125 to 0.125
- w_value: bfloat16 [2048, 256], P(('fsdp', 'ctx'), 'tp'), may hold values from -0.125 to 0.125
- w_out: bfloat16 [2048, 2048], P('tp', ('fsdp', 'ctx')), may hold values from -1 to 1
- mlp_gain: bfloat16 [2048], P(('fsdp', 'ctx')), may hold values from 0.099609375 to 1.8984375
- w_gate: bfloat16 [2048, 5632], P(('fsdp', 'ctx'), 'tp'), may hold values from -0.125 to 0.125
- w_up: bfloat16 [2048, 5632], P(('fsdp', 'ctx'), 'tp'), may hold values from -0.125 to 0.125
- w_down: bfloat16 [5632, 2048], P('tp', ('fsdp', 'ctx')), may hold values from -0.15625 to 0.15625
- cotangent: bfloat16 [4096, 2048], P(('fsdp', 'ctx')), may hold values from -6 to 6
- positions: int32 [4096], P(('fsdp', 'ctx')), may hold values from 0 to 1023, as said below
- segments: int32 [4096], P(('fsdp', 'ctx')), may hold values from 0 to 4095, as said below
Outputs:
- output: bfloat16 [4096, 2048], P(('fsdp', 'ctx'))
- input_grad: bfloat16 [4096, 2048], P(('fsdp', 'ctx'))
- attn_gain_grad: float32 [2048], P(('fsdp', 'ctx'))
- w_query_grad: float32 [2048, 2048], P(('fsdp', 'ctx'), 'tp')
- w_key_grad: float32 [2048, 256], P(('fsdp', 'ctx'), 'tp')
- w_value_grad: float32 [2048, 256], P(('fsdp', 'ctx'), 'tp')
- w_out_grad: float32 [2048, 2048], P('tp', ('fsdp', 'ctx'))
- mlp_gain_grad: float32 [2048], P(('fsdp', 'ctx'))
- w_gate_grad: float32 [2048, 5632], P(('fsdp', 'ctx'), 'tp')
- w_up_grad: float32 [2048, 5632], P(('fsdp', 'ctx'), 'tp')
- w_down_grad: float32 [5632, 2048], P('tp', ('fsdp', 'ctx'))
Inputs may be any that keep to these rules, and one draw needn't show every extreme that they name: Every sequence is cut into 8 stretches of 128 consecutive positions, laid in increasing order inside a stretch; its stretches lie on one index of fsdp, two on each index of ctx, in an order drawn from the seed; each device holds 4 stretches, those of one sequence side by side. `segments`: A document is a run of consecutive positions of one sequence with one number, 200 to 2000 long except the last of a sequence, which may be shorter; documents of different sequences have different numbers.
All inputs are finite; a program needn't handle non-finite values.
Results may differ from a plain program's by a relative error of at most 0.025.
Values may be sent and summed in bfloat16 or wider, within the bound.
A program may use at most 192 MiB of HBM per device.

v0:
```python
import jax
import jax.numpy as jnp
from jax import lax
from jax.sharding import PartitionSpec as P

H = 32
KVH = 4
HD = 64
EPSILON = 1e-05
THETA_BASE = 10000.0
MASKED_SCORE = -1e30


def shifted(value, axis, steps):
    count = lax.axis_size(axis)
    pairs = [(source, (source + steps) % count) for source in range(count)]
    return lax.ppermute(value, axis, pairs)


def rope_tables(token_pos, half_size):
    frequency = THETA_BASE ** (-jnp.arange(half_size, dtype=jnp.float32) / half_size)
    angles = token_pos.astype(jnp.float32)[:, None] * frequency[None, :]
    return (jnp.cos(angles), jnp.sin(angles))


def rotate(head_rows, cosine, sine):
    half_size = head_rows.shape[-1] // 2
    first_half = head_rows[..., :half_size]
    second_half = head_rows[..., half_size:]
    cos_rows = cosine[:, None, :]
    sin_rows = sine[:, None, :]
    return jnp.concatenate(
        [
            first_half * cos_rows - second_half * sin_rows,
            second_half * cos_rows + first_half * sin_rows,
        ],
        axis=-1,
    )


def rotate_back(head_rows, cosine, sine):
    half_size = head_rows.shape[-1] // 2
    first_half = head_rows[..., :half_size]
    second_half = head_rows[..., half_size:]
    cos_rows = cosine[:, None, :]
    sin_rows = sine[:, None, :]
    return jnp.concatenate(
        [
            first_half * cos_rows + second_half * sin_rows,
            second_half * cos_rows - first_half * sin_rows,
        ],
        axis=-1,
    )


def project(left_side, right_side):
    return jnp.dot(left_side, right_side, preferred_element_type=jnp.float32)


def project_back(left_side, right_side):
    return lax.dot_general(
        left_side, right_side, (((1,), (1,)), ((), ())), preferred_element_type=jnp.float32
    )


def weight_grad(left_side, right_side):
    return lax.dot_general(
        left_side, right_side, (((0,), (0,)), ((), ())), preferred_element_type=jnp.float32
    )


def rms_norm(rows_in, gain_vec):
    inv_rms = lax.rsqrt(jnp.mean(rows_in * rows_in, axis=-1, keepdims=True) + EPSILON)
    unit_rows = rows_in * inv_rms
    return (unit_rows * gain_vec, unit_rows, inv_rms)


def rms_norm_back(gradient, gain_vec, unit_rows, inv_rms):
    gain_grad = jnp.sum(gradient * unit_rows, axis=0)
    scaled_grad = gradient * gain_vec
    return (
        inv_rms
        * (scaled_grad - unit_rows * jnp.mean(scaled_grad * unit_rows, axis=-1, keepdims=True)),
        gain_grad,
    )


def pair_mask(query_pos, query_seg, key_pos, key_seg):
    return (query_seg[:, None] == key_seg[None, :]) & (key_pos[None, :] <= query_pos[:, None])


def split_block(kv_block, kv_heads):
    key_rows = kv_block[:, : kv_heads * HD].reshape(-1, kv_heads, HD)
    value_rows = kv_block[:, kv_heads * HD :].reshape(-1, kv_heads, HD)
    return (key_rows, value_rows)


def attend_block(state_in, queries, kv_block, visible):
    row_top, row_total, output_sum = state_in
    key_rows, value_rows = split_block(kv_block, queries.shape[1])
    scores = jnp.einsum(
        "qkgd,pkd->kgqp", queries, key_rows, preferred_element_type=jnp.float32
    ) * HD ** (-0.5)
    scores = jnp.where(visible, scores, MASKED_SCORE)
    new_top = jnp.maximum(row_top, jnp.max(scores, axis=-1))
    weights = jnp.where(visible, jnp.exp(scores - new_top[..., None]), 0.0)
    decay_factor = jnp.exp(row_top - new_top)
    row_total = row_total * decay_factor + jnp.sum(weights, axis=-1)
    mixed_heads = jnp.einsum(
        "kgqp,pkd->qkgd",
        weights.astype(jnp.bfloat16),
        value_rows,
        preferred_element_type=jnp.float32,
    )
    output_sum = output_sum * jnp.transpose(decay_factor, (2, 0, 1))[..., None] + mixed_heads
    return (new_top, row_total, output_sum)


def block_grads(queries, out_grad, kv_block, visible, log_total, delta_rows):
    key_rows, value_rows = split_block(kv_block, queries.shape[1])
    scale_factor = HD ** (-0.5)
    scores = (
        jnp.einsum("qkgd,pkd->kgqp", queries, key_rows, preferred_element_type=jnp.float32)
        * scale_factor
    )
    probs_full = jnp.where(
        visible, jnp.exp(jnp.where(visible, scores, MASKED_SCORE) - log_total[..., None]), 0.0
    )
    value_grad = jnp.einsum(
        "kgqp,qkgd->pkd",
        probs_full.astype(jnp.bfloat16),
        out_grad,
        preferred_element_type=jnp.float32,
    )
    prob_grad = jnp.einsum(
        "qkgd,pkd->kgqp", out_grad, value_rows, preferred_element_type=jnp.float32
    )
    score_grad = (probs_full * (prob_grad - delta_rows[..., None])).astype(jnp.bfloat16)
    query_grad = (
        jnp.einsum("kgqp,pkd->qkgd", score_grad, key_rows, preferred_element_type=jnp.float32)
        * scale_factor
    )
    key_grad = (
        jnp.einsum("kgqp,qkgd->pkd", score_grad, queries, preferred_element_type=jnp.float32)
        * scale_factor
    )
    block_rows = kv_block.shape[0]
    return (
        query_grad,
        jnp.concatenate(
            [key_grad.reshape(block_rows, -1), value_grad.reshape(block_rows, -1)], axis=-1
        ),
    )


def shards(
    tokens,
    attn_gain,
    w_query,
    w_key,
    w_value,
    w_out,
    mlp_gain,
    w_gate,
    w_up,
    w_down,
    cotangent,
    positions,
    segments,
):
    token_rows = tokens.shape[0]
    gain_one, query_w, key_w, value_w, out_w = (
        lax.all_gather(attn_gain, ("fsdp", "ctx"), axis=0, tiled=True),
        lax.all_gather(w_query, ("fsdp", "ctx"), axis=0, tiled=True),
        lax.all_gather(w_key, ("fsdp", "ctx"), axis=0, tiled=True),
        lax.all_gather(w_value, ("fsdp", "ctx"), axis=0, tiled=True),
        lax.all_gather(w_out, ("fsdp", "ctx"), axis=1, tiled=True),
    )
    gain_two, gate_w, up_w, down_w = (
        lax.all_gather(mlp_gain, ("fsdp", "ctx"), axis=0, tiled=True),
        lax.all_gather(w_gate, ("fsdp", "ctx"), axis=0, tiled=True),
        lax.all_gather(w_up, ("fsdp", "ctx"), axis=0, tiled=True),
        lax.all_gather(w_down, ("fsdp", "ctx"), axis=1, tiled=True),
    )
    head_count = query_w.shape[1] // HD
    kv_heads = key_w.shape[1] // HD
    groups = H // KVH
    cosine, sine = rope_tables(positions, HD // 2)
    token_float = tokens.astype(jnp.float32)
    gain_one_float = gain_one.astype(jnp.float32)
    normed_one, unit_one, inv_one = rms_norm(token_float, gain_one_float)
    normed_low = normed_one.astype(jnp.bfloat16)
    query_lin = project(normed_low, query_w)
    key_lin = project(normed_low, key_w)
    value_low = project(normed_low, value_w).astype(jnp.bfloat16)
    query_rot = rotate(query_lin.reshape(token_rows, head_count, HD), cosine, sine).astype(
        jnp.bfloat16
    )
    key_rot = rotate(key_lin.reshape(token_rows, kv_heads, HD), cosine, sine).astype(jnp.bfloat16)
    queries = query_rot.reshape(token_rows, kv_heads, groups, HD)
    kv_local = jnp.concatenate([key_rot.reshape(token_rows, kv_heads * HD), value_low], axis=-1)
    key_positions, key_segments = (
        lax.all_gather(positions, "ctx", axis=0, tiled=True),
        lax.all_gather(segments, "ctx", axis=0, tiled=True),
    )
    my_index = lax.axis_index("ctx")
    cycle_size = lax.axis_size("ctx")

    def block_marks(source):
        start_row = source * token_rows
        return pair_mask(
            positions,
            segments,
            lax.dynamic_slice_in_dim(key_positions, start_row, token_rows),
            lax.dynamic_slice_in_dim(key_segments, start_row, token_rows),
        )

    start_state = (
        jnp.full((kv_heads, groups, token_rows), MASKED_SCORE, jnp.float32),
        jnp.zeros((kv_heads, groups, token_rows), jnp.float32),
        jnp.zeros((token_rows, kv_heads, groups, HD), jnp.float32),
    )

    def forward_block(state_in, kv_block, source):
        visible = block_marks(source)
        return attend_block(state_in, queries, kv_block, visible)

    def cycle_step(state_in, step_index):
        attn_state, kv_block = state_in
        attn_state = forward_block(attn_state, kv_block, (my_index - step_index) % cycle_size)
        passed = shifted(kv_block, "ctx", 1)
        return ((attn_state, passed), kv_block)

    (attn_state, last_block), kept_blocks = lax.scan(
        cycle_step, (start_state, kv_local), jnp.arange(cycle_size - 1)
    )
    attn_state = forward_block(attn_state, last_block, (my_index + 1) % cycle_size)
    kv_blocks = jnp.concatenate([kept_blocks, last_block[None]], axis=0)
    sources = (my_index - jnp.arange(cycle_size)) % cycle_size
    row_top, row_total, output_sum = attn_state
    attended = output_sum / jnp.transpose(row_total, (2, 0, 1))[..., None]
    log_total = row_top + jnp.log(row_total)
    attended_low = attended.reshape(token_rows, head_count * HD).astype(jnp.bfloat16)
    middle = token_float + lax.psum(project(attended_low, out_w).astype(jnp.bfloat16), "tp").astype(
        jnp.float32
    )
    gain_two_float = gain_two.astype(jnp.float32)
    normed_two, unit_two, inv_two = rms_norm(middle, gain_two_float)
    normed_two_low = normed_two.astype(jnp.bfloat16)
    gate_lin = project(normed_two_low, gate_w)
    up_lin = project(normed_two_low, up_w)
    hidden_low = (jax.nn.silu(gate_lin) * up_lin).astype(jnp.bfloat16)
    result = middle + lax.psum(project(hidden_low, down_w).astype(jnp.bfloat16), "tp").astype(
        jnp.float32
    )
    output = result.astype(jnp.bfloat16)
    hidden_grad = project_back(cotangent, down_w)
    down_w_grad = weight_grad(hidden_low, cotangent)
    sigmoid_gate = jax.nn.sigmoid(gate_lin)
    gate_grad_low = (
        hidden_grad * up_lin * sigmoid_gate * (1.0 + gate_lin * (1.0 - sigmoid_gate))
    ).astype(jnp.bfloat16)
    up_grad_low = (hidden_grad * gate_lin * sigmoid_gate).astype(jnp.bfloat16)
    normed_two_grad = lax.psum(
        (project_back(gate_grad_low, gate_w) + project_back(up_grad_low, up_w)).astype(
            jnp.bfloat16
        ),
        "tp",
    ).astype(jnp.float32)
    gate_w_grad = weight_grad(normed_two_low, gate_grad_low)
    up_w_grad = weight_grad(normed_two_low, up_grad_low)
    norm_back_two, gain_two_grad = rms_norm_back(normed_two_grad, gain_two_float, unit_two, inv_two)
    middle_grad = cotangent.astype(jnp.float32) + norm_back_two
    middle_low = middle_grad.astype(jnp.bfloat16)
    attended_grad_low = project_back(middle_low, out_w).astype(jnp.bfloat16)
    out_w_grad = weight_grad(attended_low, middle_low)
    out_grad = attended_grad_low.reshape(token_rows, kv_heads, groups, HD)
    delta_rows = jnp.transpose(jnp.sum(out_grad.astype(jnp.float32) * attended, axis=-1), (1, 2, 0))

    def backward_block(kv_block, source):
        visible = block_marks(source)
        return block_grads(queries, out_grad, kv_block, visible, log_total, delta_rows)

    query_start = jnp.zeros((token_rows, kv_heads, groups, HD), jnp.float32)

    def back_step(state_in, pieces):
        query_acc, kv_acc = state_in
        query_term, kv_term = backward_block(pieces[0], pieces[1])
        passed = shifted((kv_acc + kv_term).astype(jnp.bfloat16), "ctx", 1).astype(jnp.float32)
        return ((query_acc + query_term, passed), None)

    (query_grad, kv_grad), unused = lax.scan(
        back_step, (query_start, jnp.zeros(kv_local.shape, jnp.float32)), (kv_blocks, sources)
    )
    query_grad_low = (
        rotate_back(query_grad.reshape(token_rows, head_count, HD), cosine, sine)
        .reshape(token_rows, head_count * HD)
        .astype(jnp.bfloat16)
    )
    key_grad_low = (
        rotate_back(kv_grad[:, : kv_heads * HD].reshape(token_rows, kv_heads, HD), cosine, sine)
        .reshape(token_rows, kv_heads * HD)
        .astype(jnp.bfloat16)
    )
    value_grad_low = kv_grad[:, kv_heads * HD :].astype(jnp.bfloat16)
    normed_one_grad = lax.psum(
        (
            project_back(query_grad_low, query_w)
            + project_back(key_grad_low, key_w)
            + project_back(value_grad_low, value_w)
        ).astype(jnp.bfloat16),
        "tp",
    ).astype(jnp.float32)
    query_w_grad = weight_grad(normed_low, query_grad_low)
    key_w_grad = weight_grad(normed_low, key_grad_low)
    value_w_grad = weight_grad(normed_low, value_grad_low)
    norm_back_one, gain_one_grad = rms_norm_back(normed_one_grad, gain_one_float, unit_one, inv_one)
    input_grad = (middle_grad + norm_back_one).astype(jnp.bfloat16)
    summed = (
        lax.psum_scatter(
            gain_one_grad.astype(jnp.bfloat16), ("fsdp", "ctx"), scatter_dimension=0, tiled=True
        ).astype(jnp.float32),
        lax.psum_scatter(
            query_w_grad.astype(jnp.bfloat16), ("fsdp", "ctx"), scatter_dimension=0, tiled=True
        ).astype(jnp.float32),
        lax.psum_scatter(
            key_w_grad.astype(jnp.bfloat16), ("fsdp", "ctx"), scatter_dimension=0, tiled=True
        ).astype(jnp.float32),
        lax.psum_scatter(
            value_w_grad.astype(jnp.bfloat16), ("fsdp", "ctx"), scatter_dimension=0, tiled=True
        ).astype(jnp.float32),
        lax.psum_scatter(
            out_w_grad.astype(jnp.bfloat16), ("fsdp", "ctx"), scatter_dimension=1, tiled=True
        ).astype(jnp.float32),
        lax.psum_scatter(
            gain_two_grad.astype(jnp.bfloat16), ("fsdp", "ctx"), scatter_dimension=0, tiled=True
        ).astype(jnp.float32),
        lax.psum_scatter(
            gate_w_grad.astype(jnp.bfloat16), ("fsdp", "ctx"), scatter_dimension=0, tiled=True
        ).astype(jnp.float32),
        lax.psum_scatter(
            up_w_grad.astype(jnp.bfloat16), ("fsdp", "ctx"), scatter_dimension=0, tiled=True
        ).astype(jnp.float32),
        lax.psum_scatter(
            down_w_grad.astype(jnp.bfloat16), ("fsdp", "ctx"), scatter_dimension=1, tiled=True
        ).astype(jnp.float32),
    )
    return (output, input_grad) + tuple(summed)


def solution(mesh):
    in_specs = (
        P(("fsdp", "ctx"), None),
        P(("fsdp", "ctx")),
        P(("fsdp", "ctx"), "tp"),
        P(("fsdp", "ctx"), "tp"),
        P(("fsdp", "ctx"), "tp"),
        P("tp", ("fsdp", "ctx")),
        P(("fsdp", "ctx")),
        P(("fsdp", "ctx"), "tp"),
        P(("fsdp", "ctx"), "tp"),
        P("tp", ("fsdp", "ctx")),
        P(("fsdp", "ctx"), None),
        P(("fsdp", "ctx")),
        P(("fsdp", "ctx")),
    )
    out_specs = (
        P(("fsdp", "ctx"), None),
        P(("fsdp", "ctx"), None),
        P(("fsdp", "ctx")),
        P(("fsdp", "ctx"), "tp"),
        P(("fsdp", "ctx"), "tp"),
        P(("fsdp", "ctx"), "tp"),
        P("tp", ("fsdp", "ctx")),
        P(("fsdp", "ctx")),
        P(("fsdp", "ctx"), "tp"),
        P(("fsdp", "ctx"), "tp"),
        P("tp", ("fsdp", "ctx")),
    )
    return jax.shard_map(shards, mesh=mesh, in_specs=in_specs, out_specs=out_specs, check_vma=False)
```

profile of v0, /device:TPU:0, one launch (start us, length us, event | category | flops | bytes accessed | tf_op | source)
XLA Modules:
  0.0 1101.4 jit_solution(18198275863524223515)
XLA Ops:
  8.8 9.6 all-gather.1
  19.1 7.9 all-gather.2
  27.9 12.5 %all-gather = bf16[8,1,256]{2,1,0:T(2,128)(2,1)S(1)} all-gather(bf16[1,1,256]{2,1,0:T(2,128)(2,1)S(1)} %reshape.364), channel_id=1, replica_groups=mesh['fsdp'=2,'ctx'=4,'tp'=4] {'fsdp','ctx'}, dimensions={0}, use_global_device_ids=true | all-gather | bytes 4608 | tf_op jit(solution)/shard_map/all_gather | solution.py:173
  42.5 25.8 %all_gather.34 = bf16[2048,64]{0,1:T(8,128)(2,1)S(1)} all-gather(bf16[256,64]{0,1:T(8,128)(2,1)} %param.20), channel_id=1, replica_groups=mesh['fsdp'=2,'ctx'=4,'tp'=4] {'fsdp','ctx'}, dimensions={0}, use_global_device_ids=true | all-gather | bytes 294912 | tf_op jit(solution)/shard_map/all_gather | solution.py:175
  70.4 24.0 %all_gather.35 = bf16[2048,64]{0,1:T(8,128)(2,1)S(1)} all-gather(bf16[256,64]{0,1:T(8,128)(2,1)S(1)} %copy-done.36), channel_id=1, replica_groups=mesh['fsdp'=2,'ctx'=4,'tp'=4] {'fsdp','ctx'}, dimensions={0}, use_global_device_ids=true | all-gather | bytes 294912 | tf_op jit(solution)/shard_map/all_gather | solution.py:176
  95.5 3.5 fusion.126
  100.0 45.5 %while.34 = (s32[]{:T(128)}, f32[1,8,512]{2,1,0:T(8,128)S(1)}, f32[1,8,512]{2,1,0:T(8,128)S(1)}, f32[512,1,8,64]{0,3,2,1:T(8,128)}, bf16[512,128]{0,1:T(8,128)(2...) while((s32[]{:T(128)}, f32[1,8,512]{2,1,0:T(8,128)S(1)}, ...), condition=%wide.region_4.5_spmd.clone, body=%wide.region_1.4_spmd.clone.sunk | while | flops 565731328 | bytes 63848896 | solution.py:234
  107.1 6.8 fusion.193
  114.6 2.6 collective-permute-start
  123.6 7.0 fusion.193
  137.8 7.0 fusion.193
  145.5 2.5 fusion.49
  150.7 3.2 fusion.125
  153.9 4.4 convolution_convert_fusion.5
  160.1 14.7 %all-gather.3 = bf16[8,1,256]{2,1,0:T(2,128)(2,1)S(1)} all-gather(bf16[1,1,256]{2,1,0:T(2,128)(2,1)S(1)} %reshape.370), channel_id=1, replica_groups=mesh['fsdp'=2,'ctx'=4,'tp'=4] {'fsdp','ctx'}, dimensions={0}, use_global_device_ids=true | all-gather | bytes 4608 | tf_op jit(solution)/shard_map/all_gather | solution.py:180
  174.8 71.9 %all-reduce.8.cloned.1.call-done = bf16[512,2048]{1,0:T(8,128)(2,1)} async-done(((bf16[512,2048]{1,0:T(8,128)(2,1)}), bf16[512,2048]{1,0:T(8,128)(2,1)}) %all-reduce.8.cloned.1.call-update) | async-done | bytes 2097168 | tf_op jit(solution)/shard_map/psum | solution.py:244
  246.7 2.5 multiply_reduce_fusion
  249.2 2.4 multiply_convert_fusion
  251.6 39.3 %all-gather.14.cloned.1.call-done = bf16[2048,1408]{1,0:T(8,128)(2,1)} async-done(((bf16[256,1408]{1,0:T(8,128)(2,1)}), bf16[2048,1408]{1,0:T(8,128)(2,1)}) %all-gather.14.cloned.1.call-update) | async-done | bytes 5767184 | tf_op jit(solution)/shard_map/all_gather | solution.py:181
  290.9 8.2 fusion.127
  299.1 37.0 %all-gather.16.cloned.1.call-done = bf16[2048,1408]{1,0:T(8,128)(2,1)} async-done(((bf16[256,1408]{1,0:T(8,128)(2,1)}), bf16[2048,1408]{1,0:T(8,128)(2,1)}) %all-gather.16.cloned.1.call-update) | async-done | bytes 5767184 | tf_op jit(solution)/shard_map/all_gather | solution.py:182
  336.2 8.3 fusion.128
  344.4 38.0 %all-gather.18.cloned.1.call-done = bf16[1408,2048]{1,0:T(8,128)(2,1)} async-done(((bf16[1408,256]{1,0:T(8,128)(2,1)}), bf16[1408,2048]{1,0:T(8,128)(2,1)}) %all-gather.18.cloned.1.call-update) | async-done | bytes 5767184 | tf_op jit(solution)/shard_map/all_gather | solution.py:183
  382.4 10.4 multiply_convert_fusion.1
  392.8 6.6 fusion.129
  399.5 4.7 add_convert_fusion.1
  405.8 85.0 %all-reduce.10.cloned.1.call-done = bf16[512,2048]{1,0:T(8,128)(2,1)} async-done(((bf16[512,2048]{1,0:T(8,128)(2,1)}), bf16[512,2048]{1,0:T(8,128)(2,1)}) %all-reduce.10.cloned.1.call-update) | async-done | bytes 2097168 | tf_op jit(solution)/shard_map/psum | solution.py:264
  490.9 3.9 fusion.65
  495.0 4.7 convolution_convert_fusion.9
  501.0 84.5 %while.35 = (s32[]{:T(128)}, f32[512,1,8,64]{0,3,2,1:T(8,128)}, f32[512,128]{0,1:T(8,128)S(1)}, bf16[4,512,128]{1,2,0:T(8,128)(2,1)}, s32[512]{0:T(512)S(1)}, /*...) while((s32[]{:T(128)}, f32[512,1,8,64]{0,3,2,1:T(8,128)}, ...), condition=%wide.region_14.15_spmd.clone, body=%wide.region_13.14_spmd.clone.sunk | while | flops 1369276416 | bytes 45089044 | solution.py:292
  506.8 3.4 fusion.204
  510.3 4.4 fusion.202
  519.4 2.8 collective-permute-done.1
  528.2 3.4 fusion.204
  531.6 4.4 fusion.202
  538.0 3.1 fusion.203
  549.2 3.4 fusion.204
  552.6 4.4 fusion.202
  558.6 3.1 fusion.203
  561.7 2.6 collective-permute-done.1
  570.2 3.4 fusion.204
  573.7 4.4 fusion.202
  579.7 3.1 fusion.203
  582.8 2.6 collective-permute-done.1
  585.8 2.8 convolution_convert_fusion.8
  588.7 2.8 convolution_convert_fusion.7
  591.8 6.6 convolution_convert_fusion.3
  599.8 4.2 convolution_convert_fusion.4
  604.1 7.9 convolution_convert_fusion.6
  617.1 8.0 convolution_convert_fusion.2
  625.4 7.9 convolution_convert_fusion.1
  633.4 7.7 convolution_convert_fusion
  644.4 13.2 %reduce-scatter.12.cloned.1.call-done = bf16[256,64]{0,1:T(8,128)(2,1)} async-done(((bf16[2048,64]{0,1:T(8,128)(2,1)}), bf16[256,64]{0,1:T(8,128)(2,1)}) %reduce-scatter.12.cloned.1.call-update) | async-done | bytes 32784 | tf_op jit(solution)/shard_map/reduce_scatter | solution.py:329
  659.0 43.0 %reduce-scatter.14.cloned.1.call-done = bf16[512,256]{1,0:T(8,128)(2,1)} async-done(((bf16[512,2048]{1,0:T(8,128)(2,1)}), bf16[512,256]{1,0:T(8,128)(2,1)}) %reduce-scatter.14.cloned.1.call-update) | async-done | bytes 262160 | tf_op jit(solution)/shard_map/reduce_scatter | solution.py:332
  703.8 43.1 %reduce-scatter.8.cloned.1.call-done = bf16[256,512]{1,0:T(8,128)(2,1)} async-done(((bf16[2048,512]{1,0:T(8,128)(2,1)}), bf16[256,512]{1,0:T(8,128)(2,1)}) %reduce-scatter.8.cloned.1.call-update) | async-done | bytes 262160 | tf_op jit(solution)/shard_map/reduce_scatter | solution.py:323
  748.7 156.4 %all-reduce.12.cloned.1.call-done = (bf16[512,2048]{1,0:T(8,128)(2,1)}, bf16[512,2048]{1,0:T(8,128)(2,1)}) async-done(((bf16[512,2048]{1,0:T(8,128)(2,1)}, bf16[512,2048]{1,0:T(8,128)(2,1)}), (bf16[512,2048]{1,0:T(8,128)(2,1)}, bf16[512,2048]{1,0:T(8,128)(2,1)})) %all-reduce.12.cloned.1.call-update) | async-done | bytes 4194320 | tf_op jit(solution)/shard_map/psum | solution.py:253
  905.1 2.9 fusion.69
  908.0 14.7 %all-reduce.2 = (bf16[2048]{0:T(1024)(128)(2,1)S(1)}, bf16[2048]{0:T(1024)(128)(2,1)S(1)}) all-reduce(bf16[2048]{0:T(1024)(128)(2,1)S(1)} %get-tuple-element.338, bf16[2048]{0:T(1024)(128)(2,1)S(1)} %get-tuple-element.336), channel_id=2, replica_groups=mesh['fsdp'=2,'ctx'=4,'tp'=4] {'fsdp','ctx'}, use_global_device_ids=true, to_apply=%region_18.19.clone | all-reduce | flops 4096 | bytes 16384
  923.4 8.0 fusion.61
  931.4 35.6 %reduce-scatter.16.cloned.1.call-done = bf16[256,1408]{1,0:T(8,128)(2,1)} async-done(((bf16[2048,1408]{1,0:T(8,128)(2,1)}), bf16[256,1408]{1,0:T(8,128)(2,1)}) %reduce-scatter.16.cloned.1.call-update) | async-done | bytes 720912 | tf_op jit(solution)/shard_map/reduce_scatter | solution.py:338
  969.3 60.1 %reduce-scatter.18.cloned.1.call-done = bf16[256,1408]{1,0:T(8,128)(2,1)} async-done(((bf16[2048,1408]{1,0:T(8,128)(2,1)}), bf16[256,1408]{1,0:T(8,128)(2,1)}) %reduce-scatter.18.cloned.1.call-update) | async-done | bytes 720912 | tf_op jit(solution)/shard_map/reduce_scatter | solution.py:341
  1029.4 2.3 convert_element_type.227
  1031.7 60.4 %reduce-scatter.20.cloned.1.call-done = bf16[1408,256]{1,0:T(8,128)(2,1)} async-done(((bf16[1408,2048]{1,0:T(8,128)(2,1)}), bf16[1408,256]{1,0:T(8,128)(2,1)}) %reduce-scatter.20.cloned.1.call-update) | async-done | bytes 720912 | tf_op jit(solution)/shard_map/reduce_scatter | solution.py:344
  1092.1 2.3 convert_element_type.229
  (256 shorter events, 87.7 us)
Async XLA Ops:
  7.2 61.2 %copy-start.1 = (bf16[512,2048]{1,0:T(8,128)(2,1)S(1)}, bf16[512,2048]{1,0:T(8,128)(2,1)}, u32[]{:S(2)}) copy-start(bf16[512,2048]{1,0:T(8,128)(2,1)} %param.17) | copy-start | bytes 6291460
  7.2 88.3 %all-gather.10.cloned.1.call-start = ((), (), s32[]{:S(2)}) async-start(), calls=%async_computation.7 | async-start | bytes 2359296 | tf_op jit(solution)/shard_map/all_gather | solution.py:174
  7.9 146.0 %all-gather.12.cloned.1.call-start = ((), (), s32[]{:S(2)}) async-start(), calls=%async_computation.8 | async-start | bytes 2359296 | tf_op jit(solution)/shard_map/all_gather | solution.py:177
  8.7 238.0 %all-reduce.8.cloned.1.call-start = ((), (), s32[]{:S(2)}) async-start(), calls=%async_computation.9 | async-start | bytes 4194304 | tf_op jit(solution)/shard_map/psum | solution.py:244
  8.7 61.3 %copy-start.37 = (f32[32]{0:T(128)}, f32[32]{0:T(128)S(1)}, u32[]{:S(2)}) copy-start(f32[32]{0:T(128)S(1)} %multiply_power_fusion) | copy-start | bytes 388
  19.1 50.9 %copy-start.32 = (f32[512]{0:T(512)}, f32[512]{0:T(512)S(1)}, u32[]{:S(2)}) copy-start(f32[512]{0:T(512)S(1)} %convert_element_type.186) | copy-start | bytes 6148
  40.4 29.6 %copy-start.24 = (f32[8,1,256]{2,1,0:T(1,128)}, f32[8,1,256]{2,1,0:T(1,128)S(1)}, u32[]{:S(2)}) copy-start(f32[8,1,256]{2,1,0:T(1,128)S(1)} %convert_element_type.230) | copy-start | bytes 24580
  40.4 29.9 %copy-start.36 = (bf16[256,64]{0,1:T(8,128)(2,1)S(1)}, bf16[256,64]{0,1:T(8,128)(2,1)}, u32[]{:S(2)}) copy-start(bf16[256,64]{0,1:T(8,128)(2,1)} %param.21) | copy-start | bytes 98308
  42.5 52.6 %copy-start.30 = (f32[512]{0:T(512)}, f32[512]{0:T(512)S(1)}, u32[]{:S(2)}) copy-start(f32[512]{0:T(512)S(1)} %add_rsqrt_fusion.1) | copy-start | bytes 6148
  68.3 26.8 %copy-start.6 = (bf16[2048,64]{0,1:T(8,128)(2,1)}, bf16[2048,64]{0,1:T(8,128)(2,1)S(1)}, u32[]{:S(2)}) copy-start(bf16[2048,64]{0,1:T(8,128)(2,1)S(1)} %all_gather.34) | copy-start | bytes 786436
  68.3 26.8 %copy-start.20 = (s32[512]{0:T(512)S(1)}, s32[512]{0:T(512)}, u32[]{:S(2)}) copy-start(s32[512]{0:T(512)} %param.28) | copy-start | bytes 6148
  68.3 26.8 %copy-start.22 = (s32[512]{0:T(512)S(1)}, s32[512]{0:T(512)}, u32[]{:S(2)}) copy-start(s32[512]{0:T(512)} %param.29) | copy-start | bytes 6148
  68.9 25.5 %copy-start.2 = (bf16[512,2048]{1,0:T(8,128)(2,1)}, bf16[512,2048]{1,0:T(8,128)(2,1)S(1)}, u32[]{:S(2)}) copy-start(bf16[512,2048]{1,0:T(8,128)(2,1)S(1)} %fusion.67) | copy-start | bytes 6291460
  69.2 29.8 %copy-start.15 = (f32[512,32]{0,1:T(8,128)}, f32[512,32]{0,1:T(8,128)S(1)}, u32[]{:S(2)}) copy-start(f32[512,32]{0,1:T(8,128)S(1)} %get-tuple-element.416) | copy-start | bytes 196612
  69.2 29.8 %copy-start.17 = (f32[512,32]{0,1:T(8,128)}, f32[512,32]{0,1:T(8,128)S(1)}, u32[]{:S(2)}) copy-start(f32[512,32]{0,1:T(8,128)S(1)} %get-tuple-element.417) | copy-start | bytes 196612
  100.2 14.3 %collective-permute-start = (bf16[512,128]{0,1:T(8,128)(2,1)S(1)}, bf16[512,128]{0,1:T(8,128)(2,1)S(1)}, u32[]{:S(2)}, u32[]{:S(2)}) collective-permute-start(bf16[512,128]{0,1:T(8,128)(2,1)S(1)} %copy.50), channel_id=1, source_target_pairs={{0,4},{4,8},{8,12},{12,0},{1,5},{5,9},{9,13},{13,1},{2,6},{6,10},{... | collective-permute-start | bytes 393224 | tf_op jit(solution)/shard_map/while/body/eval_jaxpr/ppermute | solution.py:17
  103.8 3.3 copy-start
  114.6 16.7 %collective-permute-start = (bf16[512,128]{0,1:T(8,128)(2,1)S(1)}, bf16[512,128]{0,1:T(8,128)(2,1)S(1)}, u32[]{:S(2)}, u32[]{:S(2)}) collective-permute-start(bf16[512,128]{0,1:T(8,128)(2,1)S(1)} %copy.50), channel_id=1, source_target_pairs={{0,4},{4,8},{8,12},{12,0},{1,5},{5,9},{9,13},{13,1},{2,6},{6,10},{... | collective-permute-start | bytes 393224 | tf_op jit(solution)/shard_map/while/body/eval_jaxpr/ppermute | solution.py:17
  120.3 3.3 copy-start
  131.3 14.2 %collective-permute-start = (bf16[512,128]{0,1:T(8,128)(2,1)S(1)}, bf16[512,128]{0,1:T(8,128)(2,1)S(1)}, u32[]{:S(2)}, u32[]{:S(2)}) collective-permute-start(bf16[512,128]{0,1:T(8,128)(2,1)S(1)} %copy.50), channel_id=1, source_target_pairs={{0,4},{4,8},{8,12},{12,0},{1,5},{5,9},{9,13},{13,1},{2,6},{6,10},{... | collective-permute-start | bytes 393224 | tf_op jit(solution)/shard_map/while/body/eval_jaxpr/ppermute | solution.py:17
  134.5 3.3 copy-start
  145.5 2.5 copy-start.28
  145.5 2.5 copy-start.29
  148.0 2.7 copy-start.41
  153.9 6.2 copy-start.40
  158.3 132.6 %all-gather.14.cloned.1.call-start = ((), (), s32[]{:S(2)}) async-start(), calls=%async_computation.10 | async-start | bytes 6488064 | tf_op jit(solution)/shard_map/all_gather | solution.py:181
  158.9 177.3 %all-gather.16.cloned.1.call-start = ((), (), s32[]{:S(2)}) async-start(), calls=%async_computation.11 | async-start | bytes 6488064 | tf_op jit(solution)/shard_map/all_gather | solution.py:182
  159.5 222.9 %all-gather.18.cloned.1.call-start = ((), (), s32[]{:S(2)}) async-start(), calls=%async_computation.12 | async-start | bytes 6488064 | tf_op jit(solution)/shard_map/all_gather | solution.py:183
  160.1 330.8 %all-reduce.10.cloned.1.call-start = ((), (), s32[]{:S(2)}) async-start(), calls=%async_computation.13 | async-start | bytes 4194304 | tf_op jit(solution)/shard_map/psum | solution.py:264
  174.8 320.0 %copy-start.26 = (f32[8,1,256]{2,1,0:T(1,128)}, f32[8,1,256]{2,1,0:T(1,128)S(1)}, u32[]{:S(2)}) copy-start(f32[8,1,256]{2,1,0:T(1,128)S(1)} %convert_element_type.231) | copy-start | bytes 24580
  246.7 2.5 copy-start.3
  249.2 245.6 %copy-start.34 = (f32[512]{0:T(512)}, f32[512]{0:T(512)S(1)}, u32[]{:S(2)}) copy-start(f32[512]{0:T(512)S(1)} %add_rsqrt_fusion) | copy-start | bytes 6148
  392.8 6.6 copy-start.44
  392.8 6.6 copy-start.43
  392.8 6.6 copy-start.39
  399.5 5.5 copy-start.19
  404.2 238.8 %reduce-scatter.10.cloned.1.call-start = ((), (), s32[]{:S(2)}) async-start(), calls=%async_computation.15 | async-start | bytes 294912 | tf_op jit(solution)/shard_map/reduce_scatter | solution.py:326
  490.8 4.0 copy-start.4
  490.9 4.0 copy-start.5
  490.9 4.1 copy-start.10
  495.0 4.7 copy-start.12
  495.0 6.0 copy-start.21
  495.0 6.0 copy-start.23
  500.9 84.5 %copy-start.33 = (f32[512]{0:T(512)S(1)}, f32[512]{0:T(512)}, u32[]{:S(2)}) copy-start(f32[512]{0:T(512)} %copy-done.32) | copy-start | bytes 6148
  501.0 84.5 %copy-start.38 = (f32[32]{0:T(128)S(1)}, f32[32]{0:T(128)}, u32[]{:S(2)}) copy-start(f32[32]{0:T(128)} %copy-done.37) | copy-start | bytes 388
  516.1 6.2 collective-permute-start.1
  537.4 5.9 collective-permute-start.1
  558.4 5.9 collective-permute-start.1
  579.5 5.9 collective-permute-start.1
  585.4 6.3 copy-start.27
  585.4 6.3 copy-start.35
  588.6 69.0 %reduce-scatter.12.cloned.1.call-start = ((), (), s32[]{:S(2)}) async-start(), calls=%async_computation.16 | async-start | bytes 294912 | tf_op jit(solution)/shard_map/reduce_scatter | solution.py:329
  591.5 6.9 copy-start.16
  591.5 6.9 copy-start.18
  591.5 110.5 %reduce-scatter.14.cloned.1.call-start = ((), (), s32[]{:S(2)}) async-start(), calls=%async_computation.17 | async-start | bytes 2359296 | tf_op jit(solution)/shard_map/reduce_scatter | solution.py:332
  598.4 148.5 %reduce-scatter.8.cloned.1.call-start = ((), (), s32[]{:S(2)}) async-start(), calls=%async_computation.14 | async-start | bytes 2359296 | tf_op jit(solution)/shard_map/reduce_scatter | solution.py:323
  604.1 301.0 %all-reduce.12.cloned.1.call-start = ((), (), s32[]{:S(2)}) async-start(), calls=%async_computation.21 | async-start | bytes 8388608 | tf_op jit(solution)/shard_map/psum | solution.py:253
  604.1 7.9 copy-start.7
  612.0 1.6 copy-start.11
  617.0 350.0 %reduce-scatter.16.cloned.1.call-start = ((), (), s32[]{:S(2)}) async-start(), calls=%async_computation.18 | async-start | bytes 6488064 | tf_op jit(solution)/shard_map/reduce_scatter | solution.py:338
  625.1 404.3 %reduce-scatter.18.cloned.1.call-start = ((), (), s32[]{:S(2)}) async-start(), calls=%async_computation.19 | async-start | bytes 6488064 | tf_op jit(solution)/shard_map/reduce_scatter | solution.py:341
  633.3 458.8 %reduce-scatter.20.cloned.1.call-start = ((), (), s32[]{:S(2)}) async-start(), calls=%async_computation.20 | async-start | bytes 6488064 | tf_op jit(solution)/shard_map/reduce_scatter | solution.py:344
  641.1 264.0 %copy-start.25 = (f32[8,1,256]{2,1,0:T(1,128)S(1)}, f32[8,1,256]{2,1,0:T(1,128)}, u32[]{:S(2)}) copy-start(f32[8,1,256]{2,1,0:T(1,128)} %copy-done.24) | copy-start | bytes 24580
  641.1 264.0 %copy-start.31 = (f32[512]{0:T(512)S(1)}, f32[512]{0:T(512)}, u32[]{:S(2)}) copy-start(f32[512]{0:T(512)} %copy-done.30) | copy-start | bytes 6148
  (5 other events, 4.5 us)
Sparse Core Ops, SparseCore 0:
  9.9 30.6 all-gather.9
  42.5 29.3 all-gather.11
  158.4 88.2 all-reduce.7
  248.6 42.2 all-gather.13
  292.8 43.3 all-gather.15
  338.0 44.3 all-gather.17
  404.3 86.4 all-reduce.9
  588.7 31.8 reduce-scatter.9
  623.9 33.5 reduce-scatter.11
  660.7 41.2 reduce-scatter.13
  705.6 41.2 reduce-scatter.7
  749.7 155.3 all-reduce.11
  908.9 58.0 reduce-scatter.15
  970.3 59.0 reduce-scatter.17
  1033.0 58.9 reduce-scatter.19
where the time goes:
time: 1110 us; the launch traced here: 1100 us
  waiting for transfers between devices  697 us (63%)
  matrix products  188 us (17%)
  blocking collectives  109 us (10%)
  other arithmetic  53.5 us (5%)
  local copies, waits for them, and re-layouts  26.4 us (2%)
  between operations  15.7 us (1%)
    psum x1, waiting for transfers between devices, shards(): lax.psum(project(hidden_low, down_w).astype(jnp.bfloat16), 'tp')  156 us
    psum x1, waiting for transfers between devices, shards(): lax.psum((project_back(gate_grad_low, gate_w) + project_back(up_grad_low,...  85 us
    psum x1, waiting for transfers between devices, shards(): lax.psum(project(attended_low, out_w).astype(jnp.bfloat16), 'tp')  71.9 us
    reduce_scatter x1, waiting for transfers between devices, shards(): lax.psum_scatter(down_w_grad.astype(jnp.bfloat16), ('fsdp', 'ctx'), scatt...  60.4 us
    reduce_scatter x1, waiting for transfers between devices, shards(): lax.psum_scatter(up_w_grad.astype(jnp.bfloat16), ('fsdp', 'ctx'), scatter...  60.1 us
    reduce_scatter x1, waiting for transfers between devices, shards(): lax.psum_scatter(query_w_grad.astype(jnp.bfloat16), ('fsdp', 'ctx'), scat...  43.1 us
    reduce_scatter x1, waiting for transfers between devices, shards(): lax.psum_scatter(out_w_grad.astype(jnp.bfloat16), ('fsdp', 'ctx'), scatte...  43 us
    dot_general x7, matrix products, weight_grad(): lax.dot_general(left_side, right_side, (((0,), (0,)), ((), ())), preferre...  39.9 us
  transfers between devices with their start and end apart: 22, of which 16 were waited for; matrix products, arithmetic and copies ran while one was open for 15% of the time, Pallas kernels for 0%

commit v1 on v0

--- a/solution.py
+++ b/solution.py
@@ -250,9 +250,9 @@
     gate_lin = project(normed_two_low, gate_w)
     up_lin = project(normed_two_low, up_w)
     hidden_low = (jax.nn.silu(gate_lin) * up_lin).astype(jnp.bfloat16)
-    result = middle + lax.psum(project(hidden_low, down_w).astype(jnp.bfloat16), "tp").astype(
-        jnp.float32
-    )
+    result = middle + jnp.sum(
+        jax.lax.all_gather(project(hidden_low, down_w).astype(jnp.bfloat16), "tp"), axis=0
+    ).astype(jnp.float32)
     output = result.astype(jnp.bfloat16)
     hidden_grad = project_back(cotangent, down_w)
     down_w_grad = weight_grad(hidden_low, cotangent)

time: 1110 us -> 1210 us (1.090)
  waiting for transfers between devices: 697 us -> 784 us
    all_gather x0 -> x1, waiting for transfers between devices: none -> 149 us  [shards(): jax.lax.all_gather(project(hidden_low, down_w).astype(jnp.bfloat16), 'tp')]
    psum x1, waiting for transfers between devices: 156 us -> 87.4 us  [shards(): lax.psum((project_back(query_grad_low, query_w) + project_back(key_grad_l...]
    reduce_scatter x1, waiting for transfers between devices: 35.6 us -> 61.1 us  [shards(): lax.psum_scatter(gate_w_grad.astype(jnp.bfloat16), ('fsdp', 'ctx'), scatt...]
    reduce_scatter x1, waiting for transfers between devices: 43 us -> 25.5 us  [shards(): lax.psum_scatter(out_w_grad.astype(jnp.bfloat16), ('fsdp', 'ctx'), scatte...]
  transfers between devices with their start and end apart: 22 -> 23, of which waited for: 16 -> 17; matrix products, arithmetic and copies ran while one was open for 15% -> 13% of each run, Pallas kernels for 0% -> 0%
where the time goes in v1:
time: 1210 us; the launch traced here: 1200 us
  waiting for transfers between devices  784 us (65%)
  matrix products  192 us (16%)
  blocking collectives  110 us (9%)
  other arithmetic  60.7 us (5%)
  local copies, waits for them, and re-layouts  25 us (2%)
  between operations  15.6 us (1%)
    all_gather x1, waiting for transfers between devices, shards(): jax.lax.all_gather(project(hidden_low, down_w).astype(jnp.bfloat16), 'tp')  149 us
    psum x1, waiting for transfers between devices, shards(): lax.psum((project_back(query_grad_low, query_w) + project_back(key_grad_l...  87.4 us
    psum x1, waiting for transfers between devices, shards(): lax.psum((project_back(gate_grad_low, gate_w) + project_back(up_grad_low,...  85 us
    psum x1, waiting for transfers between devices, shards(): lax.psum(project(attended_low, out_w).astype(jnp.bfloat16), 'tp')  71.8 us
    reduce_scatter x1, waiting for transfers between devices, shards(): lax.psum_scatter(gate_w_grad.astype(jnp.bfloat16), ('fsdp', 'ctx'), scatt...  61.1 us
    reduce_scatter x1, waiting for transfers between devices, shards(): lax.psum_scatter(down_w_grad.astype(jnp.bfloat16), ('fsdp', 'ctx'), scatt...  60.4 us
    reduce_scatter x1, waiting for transfers between devices, shards(): lax.psum_scatter(up_w_grad.astype(jnp.bfloat16), ('fsdp', 'ctx'), scatter...  60.1 us
    reduce_scatter x1, waiting for transfers between devices, shards(): lax.psum_scatter(query_w_grad.astype(jnp.bfloat16), ('fsdp', 'ctx'), scat...  42.6 us
  transfers between devices with their start and end apart: 23, of which 17 were waited for; matrix products, arithmetic and copies ran while one was open for 13% of the time, Pallas kernels for 0%

profile of v1, /device:TPU:0, one launch (start us, length us, event | category | flops | bytes accessed | tf_op | source)
XLA Modules:
  0.0 1199.1 jit_solution(11950769729936362534)
XLA Ops:
  8.8 9.6 all-gather.2
  19.1 7.9 all-gather.3
  27.9 12.5 %all-gather.1 = bf16[8,1,256]{2,1,0:T(2,128)(2,1)S(1)} all-gather(bf16[1,1,256]{2,1,0:T(2,128)(2,1)S(1)} %reshape.365), channel_id=1, replica_groups=mesh['fsdp'=2,'ctx'=4,'tp'=4] {'fsdp','ctx'}, dimensions={0}, use_global_device_ids=true | all-gather | bytes 4608 | tf_op jit(solution)/shard_map/all_gather | solution.py:173
  42.5 25.8 %all_gather.40 = bf16[2048,64]{0,1:T(8,128)(2,1)S(1)} all-gather(bf16[256,64]{0,1:T(8,128)(2,1)} %param.20), channel_id=1, replica_groups=mesh['fsdp'=2,'ctx'=4,'tp'=4] {'fsdp','ctx'}, dimensions={0}, use_global_device_ids=true | all-gather | bytes 294912 | tf_op jit(solution)/shard_map/all_gather | solution.py:175
  70.4 24.0 %all_gather.41 = bf16[2048,64]{0,1:T(8,128)(2,1)S(1)} all-gather(bf16[256,64]{0,1:T(8,128)(2,1)S(1)} %copy-done.36), channel_id=1, replica_groups=mesh['fsdp'=2,'ctx'=4,'tp'=4] {'fsdp','ctx'}, dimensions={0}, use_global_device_ids=true | all-gather | bytes 294912 | tf_op jit(solution)/shard_map/all_gather | solution.py:176
  95.5 3.5 fusion.126
  100.0 45.5 %while.34 = (s32[]{:T(128)}, f32[1,8,512]{2,1,0:T(8,128)S(1)}, f32[1,8,512]{2,1,0:T(8,128)S(1)}, f32[512,1,8,64]{0,3,2,1:T(8,128)}, bf16[512,128]{0,1:T(8,128)(2...) while((s32[]{:T(128)}, f32[1,8,512]{2,1,0:T(8,128)S(1)}, ...), condition=%wide.region_4.5_spmd.clone, body=%wide.region_1.4_spmd.clone.sunk | while | flops 565731328 | bytes 63848896 | solution.py:234
  107.2 6.8 fusion.193
  114.7 2.6 collective-permute-start
  123.7 7.0 fusion.193
  137.9 7.0 fusion.193
  150.7 3.2 fusion.125
  154.0 4.4 convolution_convert_fusion.5
  160.2 14.8 %all-gather.4 = bf16[8,1,256]{2,1,0:T(2,128)(2,1)S(1)} all-gather(bf16[1,1,256]{2,1,0:T(2,128)(2,1)S(1)} %reshape.371), channel_id=1, replica_groups=mesh['fsdp'=2,'ctx'=4,'tp'=4] {'fsdp','ctx'}, dimensions={0}, use_global_device_ids=true | all-gather | bytes 4608 | tf_op jit(solution)/shard_map/all_gather | solution.py:180
  175.0 71.8 %all-reduce.7.cloned.1.call-done = bf16[512,2048]{1,0:T(8,128)(2,1)} async-done(((bf16[512,2048]{1,0:T(8,128)(2,1)}), bf16[512,2048]{1,0:T(8,128)(2,1)}) %all-reduce.7.cloned.1.call-update) | async-done | bytes 2097168 | tf_op jit(solution)/shard_map/psum | solution.py:244
  246.8 2.5 multiply_reduce_fusion
  251.7 39.3 %all-gather.16.cloned.1.call-done = bf16[2048,1408]{1,0:T(8,128)(2,1)} async-done(((bf16[256,1408]{1,0:T(8,128)(2,1)}), bf16[2048,1408]{1,0:T(8,128)(2,1)}) %all-gather.16.cloned.1.call-update) | async-done | bytes 5767184 | tf_op jit(solution)/shard_map/all_gather | solution.py:181
  291.0 8.2 fusion.127
  299.2 37.0 %all-gather.18.cloned.1.call-done = bf16[2048,1408]{1,0:T(8,128)(2,1)} async-done(((bf16[256,1408]{1,0:T(8,128)(2,1)}), bf16[2048,1408]{1,0:T(8,128)(2,1)}) %all-gather.18.cloned.1.call-update) | async-done | bytes 5767184 | tf_op jit(solution)/shard_map/all_gather | solution.py:182
  336.2 8.3 fusion.128
  344.5 38.0 %all-gather.20.cloned.1.call-done = bf16[1408,2048]{1,0:T(8,128)(2,1)} async-done(((bf16[1408,256]{1,0:T(8,128)(2,1)}), bf16[1408,2048]{1,0:T(8,128)(2,1)}) %all-gather.20.cloned.1.call-update) | async-done | bytes 5767184 | tf_op jit(solution)/shard_map/all_gather | solution.py:183
  382.5 10.4 multiply_convert_fusion.1
  392.9 6.6 fusion.129
  399.5 4.7 add_convert_fusion.1
  405.9 85.0 %all-reduce.9.cloned.1.call-done = bf16[512,2048]{1,0:T(8,128)(2,1)} async-done(((bf16[512,2048]{1,0:T(8,128)(2,1)}), bf16[512,2048]{1,0:T(8,128)(2,1)}) %all-reduce.9.cloned.1.call-update) | async-done | bytes 2097168 | tf_op jit(solution)/shard_map/psum | solution.py:264
  490.9 3.9 fusion.65
  495.0 4.7 convolution_convert_fusion.9
  501.1 84.5 %while.35 = (s32[]{:T(128)}, f32[512,1,8,64]{0,3,2,1:T(8,128)}, f32[512,128]{0,1:T(8,128)S(1)}, bf16[4,512,128]{1,2,0:T(8,128)(2,1)}, s32[512]{0:T(512)S(1)}, /*...) while((s32[]{:T(128)}, f32[512,1,8,64]{0,3,2,1:T(8,128)}, ...), condition=%wide.region_14.15_spmd.clone, body=%wide.region_13.14_spmd.clone.sunk | while | flops 1369276416 | bytes 45089044 | solution.py:292
  507.0 3.4 fusion.204
  510.4 4.3 fusion.202
  519.6 2.8 collective-permute-done.1
  528.3 3.4 fusion.204
  531.7 4.3 fusion.202
  538.1 3.1 fusion.203
  549.4 3.4 fusion.204
  552.8 4.4 fusion.202
  558.8 3.1 fusion.203
  561.9 2.6 collective-permute-done.1
  570.4 3.4 fusion.204
  573.9 4.3 fusion.202
  579.9 3.1 fusion.203
  583.0 2.6 collective-permute-done.1
  585.7 2.8 convolution_convert_fusion.7
  588.8 2.8 convolution_convert_fusion.8
  593.3 2.8 fusion.110
  596.2 3.1 fusion.130
  601.4 6.5 convolution_convert_fusion.3
  608.0 4.2 convolution_convert_fusion.4
  612.3 8.0 convolution_convert_fusion.2
  620.8 7.9 convolution_convert_fusion.1
  628.8 7.7 convolution_convert_fusion
  636.6 7.9 convolution_convert_fusion.6
  647.2 13.4 %reduce-scatter.12.cloned.1.call-done = bf16[256,64]{0,1:T(8,128)(2,1)} async-done(((bf16[2048,64]{0,1:T(8,128)(2,1)}), bf16[256,64]{0,1:T(8,128)(2,1)}) %reduce-scatter.12.cloned.1.call-update) | async-done | bytes 32784 | tf_op jit(solution)/shard_map/reduce_scatter | solution.py:329
  662.0 87.4 %all-reduce.11.cloned.1.call-done = bf16[512,2048]{1,0:T(8,128)(2,1)} async-done(((bf16[512,2048]{1,0:T(8,128)(2,1)}), bf16[512,2048]{1,0:T(8,128)(2,1)}) %all-reduce.11.cloned.1.call-update) | async-done | bytes 2097168 | tf_op jit(solution)/shard_map/psum | solution.py:306
  749.3 2.9 fusion.69
  752.2 14.8 %all-reduce.2 = (bf16[2048]{0:T(1024)(128)(2,1)S(1)}, bf16[2048]{0:T(1024)(128)(2,1)S(1)}) all-reduce(bf16[2048]{0:T(1024)(128)(2,1)S(1)} %get-tuple-element.338, bf16[2048]{0:T(1024)(128)(2,1)S(1)} %get-tuple-element.336), channel_id=3, replica_groups=mesh['fsdp'=2,'ctx'=4,'tp'=4] {'fsdp','ctx'}, use_global_device_ids=true, to_apply=%region_18.19.clone | all-reduce | flops 4096 | bytes 16384
  767.7 25.5 %reduce-scatter.14.cloned.1.call-done = bf16[512,256]{1,0:T(8,128)(2,1)} async-done(((bf16[512,2048]{1,0:T(8,128)(2,1)}), bf16[512,256]{1,0:T(8,128)(2,1)}) %reduce-scatter.14.cloned.1.call-update) | async-done | bytes 262160 | tf_op jit(solution)/shard_map/reduce_scatter | solution.py:332
  795.0 42.6 %reduce-scatter.8.cloned.1.call-done = bf16[256,512]{1,0:T(8,128)(2,1)} async-done(((bf16[2048,512]{1,0:T(8,128)(2,1)}), bf16[256,512]{1,0:T(8,128)(2,1)}) %reduce-scatter.8.cloned.1.call-update) | async-done | bytes 262160 | tf_op jit(solution)/shard_map/reduce_scatter | solution.py:323
  839.4 61.1 %reduce-scatter.16.cloned.1.call-done = bf16[256,1408]{1,0:T(8,128)(2,1)} async-done(((bf16[2048,1408]{1,0:T(8,128)(2,1)}), bf16[256,1408]{1,0:T(8,128)(2,1)}) %reduce-scatter.16.cloned.1.call-update) | async-done | bytes 720912 | tf_op jit(solution)/shard_map/reduce_scatter | solution.py:338
  902.8 60.1 %reduce-scatter.18.cloned.1.call-done = bf16[256,1408]{1,0:T(8,128)(2,1)} async-done(((bf16[2048,1408]{1,0:T(8,128)(2,1)}), bf16[256,1408]{1,0:T(8,128)(2,1)}) %reduce-scatter.18.cloned.1.call-update) | async-done | bytes 720912 | tf_op jit(solution)/shard_map/reduce_scatter | solution.py:341
  965.1 60.4 %reduce-scatter.20.cloned.1.call-done = bf16[1408,256]{1,0:T(8,128)(2,1)} async-done(((bf16[1408,2048]{1,0:T(8,128)(2,1)}), bf16[1408,256]{1,0:T(8,128)(2,1)}) %reduce-scatter.20.cloned.1.call-update) | async-done | bytes 720912 | tf_op jit(solution)/shard_map/reduce_scatter | solution.py:344
  1027.9 149.3 %all-gather.22.cloned.1.call-done = bf16[2048,2048]{1,0:T(8,128)(2,1)} async-done(((bf16[512,2048]{1,0:T(8,128)(2,1)}), bf16[2048,2048]{1,0:T(8,128)(2,1)}) %all-gather.22.cloned.1.call-update) | async-done | bytes 8388624 | tf_op jit(solution)/shard_map/all_gather | solution.py:254
  1177.2 7.2 reduce_sum.103
  1184.4 8.0 fusion.61
  (260 shorter events, 94.0 us)
Async XLA Ops:
  7.2 61.2 %copy-start.1 = (bf16[512,2048]{1,0:T(8,128)(2,1)S(1)}, bf16[512,2048]{1,0:T(8,128)(2,1)}, u32[]{:S(2)}) copy-start(bf16[512,2048]{1,0:T(8,128)(2,1)} %param.17) | copy-start | bytes 6291460
  7.2 88.3 %all-gather.12.cloned.1.call-start = ((), (), s32[]{:S(2)}) async-start(), calls=%async_computation.7 | async-start | bytes 2359296 | tf_op jit(solution)/shard_map/all_gather | solution.py:174
  7.9 146.1 %all-gather.14.cloned.1.call-start = ((), (), s32[]{:S(2)}) async-start(), calls=%async_computation.8 | async-start | bytes 2359296 | tf_op jit(solution)/shard_map/all_gather | solution.py:177
  8.7 238.1 %all-reduce.7.cloned.1.call-start = ((), (), s32[]{:S(2)}) async-start(), calls=%async_computation.9 | async-start | bytes 4194304 | tf_op jit(solution)/shard_map/psum | solution.py:244
  8.7 61.3 %copy-start.37 = (f32[32]{0:T(128)}, f32[32]{0:T(128)S(1)}, u32[]{:S(2)}) copy-start(f32[32]{0:T(128)S(1)} %multiply_power_fusion) | copy-start | bytes 388
  19.1 50.9 %copy-start.32 = (f32[512]{0:T(512)}, f32[512]{0:T(512)S(1)}, u32[]{:S(2)}) copy-start(f32[512]{0:T(512)S(1)} %convert_element_type.188) | copy-start | bytes 6148
  40.4 29.6 %copy-start.24 = (f32[8,1,256]{2,1,0:T(1,128)}, f32[8,1,256]{2,1,0:T(1,128)S(1)}, u32[]{:S(2)}) copy-start(f32[8,1,256]{2,1,0:T(1,128)S(1)} %convert_element_type.232) | copy-start | bytes 24580
  40.4 29.9 %copy-start.36 = (bf16[256,64]{0,1:T(8,128)(2,1)S(1)}, bf16[256,64]{0,1:T(8,128)(2,1)}, u32[]{:S(2)}) copy-start(bf16[256,64]{0,1:T(8,128)(2,1)} %param.21) | copy-start | bytes 98308
  42.5 52.6 %copy-start.30 = (f32[512]{0:T(512)}, f32[512]{0:T(512)S(1)}, u32[]{:S(2)}) copy-start(f32[512]{0:T(512)S(1)} %add_rsqrt_fusion.1) | copy-start | bytes 6148
  68.3 26.8 %copy-start.9 = (bf16[2048,64]{0,1:T(8,128)(2,1)}, bf16[2048,64]{0,1:T(8,128)(2,1)S(1)}, u32[]{:S(2)}) copy-start(bf16[2048,64]{0,1:T(8,128)(2,1)S(1)} %all_gather.40) | copy-start | bytes 786436
  68.3 26.8 %copy-start.20 = (s32[512]{0:T(512)S(1)}, s32[512]{0:T(512)}, u32[]{:S(2)}) copy-start(s32[512]{0:T(512)} %param.28) | copy-start | bytes 6148
  68.3 26.8 %copy-start.22 = (s32[512]{0:T(512)S(1)}, s32[512]{0:T(512)}, u32[]{:S(2)}) copy-start(s32[512]{0:T(512)} %param.29) | copy-start | bytes 6148
  68.9 25.5 %copy-start.2 = (bf16[512,2048]{1,0:T(8,128)(2,1)}, bf16[512,2048]{1,0:T(8,128)(2,1)S(1)}, u32[]{:S(2)}) copy-start(bf16[512,2048]{1,0:T(8,128)(2,1)S(1)} %fusion.67) | copy-start | bytes 6291460
  69.2 29.8 %copy-start.15 = (f32[512,32]{0,1:T(8,128)}, f32[512,32]{0,1:T(8,128)S(1)}, u32[]{:S(2)}) copy-start(f32[512,32]{0,1:T(8,128)S(1)} %get-tuple-element.414) | copy-start | bytes 196612
  69.2 29.8 %copy-start.17 = (f32[512,32]{0,1:T(8,128)}, f32[512,32]{0,1:T(8,128)S(1)}, u32[]{:S(2)}) copy-start(f32[512,32]{0,1:T(8,128)S(1)} %get-tuple-element.415) | copy-start | bytes 196612
  100.3 14.3 %collective-permute-start = (bf16[512,128]{0,1:T(8,128)(2,1)S(1)}, bf16[512,128]{0,1:T(8,128)(2,1)S(1)}, u32[]{:S(2)}, u32[]{:S(2)}) collective-permute-start(bf16[512,128]{0,1:T(8,128)(2,1)S(1)} %copy.50), channel_id=1, source_target_pairs={{0,4},{4,8},{8,12},{12,0},{1,5},{5,9},{9,13},{13,1},{2,6},{6,10},{... | collective-permute-start | bytes 393224 | tf_op jit(solution)/shard_map/while/body/eval_jaxpr/ppermute | solution.py:17
  103.9 3.3 copy-start
  114.7 16.7 %collective-permute-start = (bf16[512,128]{0,1:T(8,128)(2,1)S(1)}, bf16[512,128]{0,1:T(8,128)(2,1)S(1)}, u32[]{:S(2)}, u32[]{:S(2)}) collective-permute-start(bf16[512,128]{0,1:T(8,128)(2,1)S(1)} %copy.50), channel_id=1, source_target_pairs={{0,4},{4,8},{8,12},{12,0},{1,5},{5,9},{9,13},{13,1},{2,6},{6,10},{... | collective-permute-start | bytes 393224 | tf_op jit(solution)/shard_map/while/body/eval_jaxpr/ppermute | solution.py:17
  120.4 3.3 copy-start
  131.3 14.2 %collective-permute-start = (bf16[512,128]{0,1:T(8,128)(2,1)S(1)}, bf16[512,128]{0,1:T(8,128)(2,1)S(1)}, u32[]{:S(2)}, u32[]{:S(2)}) collective-permute-start(bf16[512,128]{0,1:T(8,128)(2,1)S(1)} %copy.50), channel_id=1, source_target_pairs={{0,4},{4,8},{8,12},{12,0},{1,5},{5,9},{9,13},{13,1},{2,6},{6,10},{... | collective-permute-start | bytes 393224 | tf_op jit(solution)/shard_map/while/body/eval_jaxpr/ppermute | solution.py:17
  134.6 3.3 copy-start
  145.5 2.5 copy-start.29
  148.0 2.7 copy-start.41
  154.0 6.2 copy-start.40
  158.4 132.6 %all-gather.16.cloned.1.call-start = ((), (), s32[]{:S(2)}) async-start(), calls=%async_computation.10 | async-start | bytes 6488064 | tf_op jit(solution)/shard_map/all_gather | solution.py:181
  159.0 177.2 %all-gather.18.cloned.1.call-start = ((), (), s32[]{:S(2)}) async-start(), calls=%async_computation.11 | async-start | bytes 6488064 | tf_op jit(solution)/shard_map/all_gather | solution.py:182
  159.5 222.9 %all-gather.20.cloned.1.call-start = ((), (), s32[]{:S(2)}) async-start(), calls=%async_computation.12 | async-start | bytes 6488064 | tf_op jit(solution)/shard_map/all_gather | solution.py:183
  160.1 330.8 %all-reduce.9.cloned.1.call-start = ((), (), s32[]{:S(2)}) async-start(), calls=%async_computation.13 | async-start | bytes 4194304 | tf_op jit(solution)/shard_map/psum | solution.py:264
  175.0 319.9 %copy-start.26 = (f32[8,1,256]{2,1,0:T(1,128)}, f32[8,1,256]{2,1,0:T(1,128)S(1)}, u32[]{:S(2)}) copy-start(f32[8,1,256]{2,1,0:T(1,128)S(1)} %convert_element_type.233) | copy-start | bytes 24580
  246.8 2.5 copy-start.3
  249.3 245.6 %copy-start.34 = (f32[512]{0:T(512)}, f32[512]{0:T(512)S(1)}, u32[]{:S(2)}) copy-start(f32[512]{0:T(512)S(1)} %add_rsqrt_fusion) | copy-start | bytes 6148
  392.9 6.6 copy-start.44
  392.9 6.6 copy-start.43
  392.9 6.6 copy-start.39
  399.5 5.6 copy-start.19
  404.2 241.5 %reduce-scatter.10.cloned.1.call-start = ((), (), s32[]{:S(2)}) async-start(), calls=%async_computation.16 | async-start | bytes 294912 | tf_op jit(solution)/shard_map/reduce_scatter | solution.py:326
  490.9 4.0 copy-start.4
  490.9 4.0 copy-start.6
  490.9 4.1 copy-start.11
  495.0 4.7 copy-start.12
  495.0 6.0 copy-start.21
  495.0 6.0 copy-start.23
  501.0 87.5 %copy-start.33 = (f32[512]{0:T(512)S(1)}, f32[512]{0:T(512)}, u32[]{:S(2)}) copy-start(f32[512]{0:T(512)} %copy-done.32) | copy-start | bytes 6148
  501.1 87.4 %copy-start.38 = (f32[32]{0:T(128)S(1)}, f32[32]{0:T(128)}, u32[]{:S(2)}) copy-start(f32[32]{0:T(128)} %copy-done.37) | copy-start | bytes 388
  516.2 6.2 collective-permute-start.1
  537.5 5.9 collective-permute-start.1
  558.6 5.9 collective-permute-start.1
  579.7 5.9 collective-permute-start.1
  585.6 6.3 copy-start.16
  585.6 6.3 copy-start.18
  585.6 7.7 copy-start.10
  591.6 68.9 %reduce-scatter.12.cloned.1.call-start = ((), (), s32[]{:S(2)}) async-start(), calls=%async_computation.17 | async-start | bytes 294912 | tf_op jit(solution)/shard_map/reduce_scatter | solution.py:329
  596.1 153.2 %all-reduce.11.cloned.1.call-start = ((), (), s32[]{:S(2)}) async-start(), calls=%async_computation.14 | async-start | bytes 4194304 | tf_op jit(solution)/shard_map/psum | solution.py:306
  596.2 3.1 copy-start.5
  596.2 3.1 copy-start.8
  601.4 191.8 %reduce-scatter.14.cloned.1.call-start = ((), (), s32[]{:S(2)}) async-start(), calls=%async_computation.18 | async-start | bytes 2359296 | tf_op jit(solution)/shard_map/reduce_scatter | solution.py:332
  608.0 229.6 %reduce-scatter.8.cloned.1.call-start = ((), (), s32[]{:S(2)}) async-start(), calls=%async_computation.15 | async-start | bytes 2359296 | tf_op jit(solution)/shard_map/reduce_scatter | solution.py:323
  612.3 288.2 %reduce-scatter.16.cloned.1.call-start = ((), (), s32[]{:S(2)}) async-start(), calls=%async_computation.19 | async-start | bytes 6488064 | tf_op jit(solution)/shard_map/reduce_scatter | solution.py:338
  620.4 342.5 %reduce-scatter.18.cloned.1.call-start = ((), (), s32[]{:S(2)}) async-start(), calls=%async_computation.20 | async-start | bytes 6488064 | tf_op jit(solution)/shard_map/reduce_scatter | solution.py:341
  628.7 396.8 %reduce-scatter.20.cloned.1.call-start = ((), (), s32[]{:S(2)}) async-start(), calls=%async_computation.21 | async-start | bytes 6488064 | tf_op jit(solution)/shard_map/reduce_scatter | solution.py:344
  636.5 8.0 copy-start.42
  636.6 112.8 %copy-start.25 = (f32[8,1,256]{2,1,0:T(1,128)S(1)}, f32[8,1,256]{2,1,0:T(1,128)}, u32[]{:S(2)}) copy-start(f32[8,1,256]{2,1,0:T(1,128)} %copy-done.24) | copy-start | bytes 24580
  636.6 112.8 %copy-start.31 = (f32[512]{0:T(512)S(1)}, f32[512]{0:T(512)}, u32[]{:S(2)}) copy-start(f32[512]{0:T(512)} %copy-done.30) | copy-start | bytes 6148
  636.6 540.7 %all-gather.22.cloned.1.call-start = ((), (), s32[]{:S(2)}) async-start(), calls=%async_computation.22 | async-start | bytes 10485760 | tf_op jit(solution)/shard_map/all_gather | solution.py:254
  (6 other events, 9.3 us)
Sparse Core Ops, SparseCore 0:
  9.9 30.6 all-gather.11
  42.5 29.3 all-gather.13
  158.5 88.2 all-reduce.6
  248.7 42.2 all-gather.15
  292.8 43.3 all-gather.17
  338.1 44.3 all-gather.19
  404.4 86.5 all-reduce.8
  591.7 31.8 reduce-scatter.9
  626.9 33.5 reduce-scatter.11
  662.8 86.5 all-reduce.10
  753.0 40.1 reduce-scatter.13
  796.3 41.1 reduce-scatter.7
  841.4 59.0 reduce-scatter.15
  903.8 59.0 reduce-scatter.17
  966.5 58.9 reduce-scatter.19
  1027.6 149.6 all-gather.21
